TPU v7x, 32 devices: a whole 2x2x4 slice. The times are simulated.
32 devices in a mesh: ctx: 2 (over x), tp: 4 (over y, core), pp: 4 (over z).
Axes of the slice: x: 2, y: 2, z: 4, core: 2. Of those that a mesh axis runs over, the one named last changes fastest.
Arguments:
- lin_query: bfloat16 [4, 512, 8192], P('pp', 'ctx', 'tp'), may hold values from -6 to 6
- lin_key: bfloat16 [4, 512, 8192], P('pp', 'ctx', 'tp'), may hold values from -6 to 6
- lin_value: bfloat16 [4, 512, 8192], P('pp', 'ctx', 'tp'), may hold values from -6 to 6
- log_decay: float32 [4, 512, 64], P('pp', 'ctx', 'tp'), may hold values from -1 to 0, as said below
- out_gate: bfloat16 [4, 512, 8192], P('pp', 'ctx', 'tp'), may hold values from -6 to 6
- norm_gain: float32 [4, 8192], P('pp', 'tp'), may hold values from 0.1 to 1.9
- soft_query: bfloat16 [4, 512, 8192], P('pp', 'ctx', 'tp'), may hold values from -5 to 5
- soft_key: bfloat16 [4, 512, 1024], P('pp', 'ctx', 'tp'), may hold values from -5 to 5
- soft_value: bfloat16 [4, 512, 1024], P('pp', 'ctx', 'tp'), may hold values from -6 to 6
Outputs:
- lin_handed: bfloat16 [4, 512, 8192], P('pp', 'ctx', 'tp')
- soft_handed: bfloat16 [4, 512, 8192], P('pp', 'ctx', 'tp')
Inputs may be any that keep to these rules, and one draw needn't show every extreme that they name: `log_decay`: negative everywhere.
All inputs are finite; a program needn't handle non-finite values.
Results may differ from a plain program's by a relative error of at most 0.0049.
Values may be sent and summed in bfloat16 or wider, within the bound.
No kernel may reach another device: no remote copies, remote signals or barrier semaphores. Data moves between devices by JAX's collectives and lax.ppermute only.
A program may use at most 128 MiB of HBM per device.

v0:
```python
import math
import jax
import jax.numpy as jnp
from jax import lax
from jax.sharding import PartitionSpec as P

HEADS = 64
KV_HEADS = 8
HD = 128
BLK = 256
epsilon = 1e-06
lowest = -1e30


def passed_along(block, axis, distance):
    devices = range(lax.axis_size(axis))
    route = [((i - distance) % len(devices), i) for i in devices]
    return lax.ppermute(block, axis, route)


def lightning_local(query_rows, key_rows, value_rows, decays):
    length, head_count = decays.shape
    blocks = length // BLK
    queries = query_rows.reshape(blocks, BLK, head_count, HD)
    keys_all = key_rows.reshape(blocks, BLK, head_count, HD)
    values_all = value_rows.reshape(blocks, BLK, head_count, HD)
    running_log = jnp.cumsum(decays.reshape(blocks, BLK, head_count), axis=1)
    closing_log = running_log[:, -1, :]
    scores = jnp.einsum("bthd,bshd->bhts", queries, keys_all, preferred_element_type=jnp.float32)
    log_turned = jnp.swapaxes(running_log, 1, 2)
    log_gap = log_turned[:, :, :, None] - log_turned[:, :, None, :]
    causal = lax.iota(jnp.int32, BLK)[:, None] >= lax.iota(jnp.int32, BLK)[None, :]
    decay_mask = jnp.where(causal, jnp.exp(jnp.where(causal, log_gap, 0.0)), 0.0)
    weights = (scores * decay_mask).astype(jnp.bfloat16)
    inside = jnp.einsum("bhts,bshd->bthd", weights, values_all, preferred_element_type=jnp.float32)
    pressed = (
        keys_all.astype(jnp.float32) * jnp.exp(closing_log[:, None, :] - running_log)[..., None]
    ).astype(jnp.bfloat16)
    updates = jnp.einsum("bshd,bshe->bhde", pressed, values_all, preferred_element_type=jnp.float32)

    def advance(state, inputs):
        factor_log, update = inputs
        return (jnp.exp(factor_log)[:, None, None] * state + update, state)

    closing, before = lax.scan(
        advance, jnp.zeros((head_count, HD, HD), jnp.float32), (closing_log, updates)
    )
    lifted = queries.astype(jnp.float32) * jnp.exp(running_log)[..., None]
    earlier_part = jnp.einsum("bthd,bhde->bthe", lifted, before, precision=lax.Precision.HIGHEST)
    offsets = jnp.cumsum(closing_log, axis=0) - closing_log
    carried = lifted * jnp.exp(offsets)[:, None, :, None]
    return (inside + earlier_part, carried, closing, jnp.sum(closing_log, axis=0))


def absorb(running, query_rows, row_pos, key_rows, value_rows, key_pos):
    row_peak, totals, weighted = running
    scores = jnp.einsum(
        "tkgd,skd->tkgs", query_rows, key_rows, preferred_element_type=jnp.float32
    ) * HD ** (-0.5)
    causal = (row_pos[:, None] >= key_pos[None, :])[:, None, None, :]
    block_peak = jnp.max(jnp.where(causal, scores, lowest), axis=-1)
    new_peak = jnp.maximum(row_peak, block_peak)
    unscaled = jnp.where(causal, jnp.exp(scores - new_peak[..., None]), 0.0)
    shrink = jnp.exp(row_peak - new_peak)
    totals = shrink * totals + jnp.sum(unscaled, axis=-1)
    weighted = shrink[..., None] * weighted + jnp.einsum(
        "tkgs,skd->tkgd",
        unscaled.astype(jnp.bfloat16),
        value_rows,
        preferred_element_type=jnp.float32,
    )
    return (new_peak, totals, weighted)


def empty_state(length, kv_count, group_size):
    return (
        jnp.full((length, kv_count, group_size), lowest, jnp.float32),
        jnp.zeros((length, kv_count, group_size), jnp.float32),
        jnp.zeros((length, kv_count, group_size, HD), jnp.float32),
    )


def local(
    lin_query, lin_key, lin_value, log_decay, out_gate, norm_gain, soft_query, soft_key, soft_value
):
    length = lin_query.shape[1]
    head_count = log_decay.shape[2]
    kv_count = soft_key.shape[2] // HD
    group_size = HEADS // KV_HEADS
    position = lax.axis_index("ctx")
    local_part, carried, closing, device_log = lightning_local(
        lin_query[0], lin_key[0], lin_value[0], log_decay[0]
    )
    gathered_states, device_logs = (
        lax.all_gather(closing[None], "ctx", axis=0, tiled=True),
        lax.all_gather(device_log[None, :], "ctx", axis=0, tiled=True),
    )
    devices = device_logs.shape[0]
    rising = jnp.cumsum(device_logs, axis=0)
    owners = lax.iota(jnp.int32, devices)
    earlier_mask = (owners < position)[:, None]
    reached = jnp.sum(jnp.where(earlier_mask, device_logs, 0.0), axis=0)
    weight = jnp.where(
        earlier_mask, jnp.exp(jnp.where(earlier_mask, reached[None, :] - rising, 0.0)), 0.0
    )
    incoming = jnp.einsum("jh,jhde->hde", weight, gathered_states, precision=lax.Precision.HIGHEST)
    arrived = jnp.einsum("bthd,hde->bthe", carried, incoming, precision=lax.Precision.HIGHEST)
    mixture = (local_part + arrived).reshape(length, head_count, HD)
    normed = mixture * lax.rsqrt(jnp.mean(mixture * mixture, axis=-1, keepdims=True) + epsilon)
    lin_out = (
        normed.reshape(length, head_count * HD)
        * norm_gain[0][None, :]
        * jax.nn.sigmoid(out_gate[0].astype(jnp.float32))
    ).astype(jnp.bfloat16)
    query_rows = soft_query[0].reshape(length, kv_count, group_size, HD)
    key_rows = soft_key[0].reshape(length, kv_count, HD)
    value_rows = soft_value[0].reshape(length, kv_count, HD)
    row_pos = position * length + lax.iota(jnp.int32, length)
    last_row = position * length + length - 1
    key_piece = lax.all_gather(key_rows, "ctx", axis=0, tiled=True)
    value_piece = lax.all_gather(value_rows, "ctx", axis=0, tiled=True)
    piece_rows = key_piece.shape[0]
    stride = math.gcd(piece_rows, 512)

    def absorb_block(turn, kept):
        offset = turn * stride
        key_part = lax.dynamic_slice_in_dim(key_piece, offset, stride, 0)
        value_part = lax.dynamic_slice_in_dim(value_piece, offset, stride, 0)
        key_pos = offset + lax.iota(jnp.int32, stride)
        return absorb(kept, query_rows, row_pos, key_part, value_part, key_pos)

    def work_all(kept):
        return lax.fori_loop(0, piece_rows // stride, absorb_block, kept)

    def skip_all(kept):
        return kept

    row_peak, totals, weighted = lax.cond(
        jnp.int32(0) <= last_row, work_all, skip_all, empty_state(length, kv_count, group_size)
    )
    soft_out = (weighted / totals[..., None]).astype(jnp.bfloat16).reshape(length, head_count * HD)
    lin_handed, soft_handed = passed_along((lin_out[None], soft_out[None]), "pp", 1)
    return (lin_handed, soft_handed)


def solution(mesh):
    return jax.shard_map(
        local,
        mesh=mesh,
        in_specs=(
            P("pp", "ctx", "tp"),
            P("pp", "ctx", "tp"),
            P("pp", "ctx", "tp"),
            P("pp", "ctx", "tp"),
            P("pp", "ctx", "tp"),
            P("pp", "tp"),
            P("pp", "ctx", "tp"),
            P("pp", "ctx", "tp"),
            P("pp", "ctx", "tp"),
        ),
        out_specs=(P("pp", "ctx", "tp"), P("pp", "ctx", "tp")),
        check_vma=False,
    )
```

profile of v0, /device:TPU:0, one launch (start us, length us, event | category | flops | bytes accessed | tf_op | source)
XLA Modules:
  0.0 104.8 jit_solution(13572819028677515258)
XLA Ops:
  9.3 1.5 %copy.98 = bf16[1,256,2048]{1,2,0:T(8,128)(2,1)S(1)} copy(bf16[1,256,2048]{2,1,0:T(8,128)(2,1)} %param.12) | data formatting | bytes 2097152 | tf_op jit(solution)/shard_map/reshape.8
  10.8 1.3 %copy.104 = bf16[32,8,16,128]{3,2,1,0:T(8,128)(2,1)} copy(bf16[32,8,16,128]{3,1,2,0:T(8,128)(2,1)S(1)} %bitcast.100) | data formatting | bytes 2097152
  12.1 2.8 %convolution_add_fusion = f32[16,128,128]{2,1,0:T(8,128)} fusion(bf16[256,16,128]{0,2,1:T(8,128)(2,1)S(1)} %bitcast.103, f32[256,16]{0,1:T(8,128)S(1)} %bitcast.113, bf16[256,16,128]{2,1,0:T(8,128)(2,1)} %bitcast.49, f32[16]{0:T(128)S(1)} %get-tuple-element.92), kind=kOutput, calls=%fused_computation.34 | convolution fusion | flops 136052736 | bytes 3162176 | tf_op jit(solution)/shard_map/bshd,bshe->bhde/dot_general | solution.py:39
  15.3 7.1 %all_gather.14 = bf16[512,2,128]{0,2,1:T(8,128)(2,1)S(1)} all-gather(bf16[256,2,128]{0,2,1:T(8,128)(2,1)S(1)} %bitcast.106), channel_id=1, replica_groups=mesh['ctx'=2,'tp'=4,'pp'=4] {'ctx'}, dimensions={0}, use_global_device_ids=true | all-gather | bytes 393216 | tf_op jit(solution)/shard_map/all_gather | solution.py:120
  22.4 7.4 %all_gather.15 = bf16[512,2,128]{0,2,1:T(8,128)(2,1)S(1)} all-gather(bf16[256,2,128]{0,2,1:T(8,128)(2,1)S(1)} %bitcast.105), channel_id=1, replica_groups=mesh['ctx'=2,'tp'=4,'pp'=4] {'ctx'}, dimensions={0}, use_global_device_ids=true | all-gather | bytes 393216 | tf_op jit(solution)/shard_map/all_gather | solution.py:121
  29.7 6.3 %conditional.1 = (f32[256,2,8]{0,2,1:T(8,128)S(1)}, f32[256,2,8,128]{3,0,2,1:T(8,128)S(1)}) conditional(s32[]{:T(128)} %convert_element_type.48, () %tuple.20, (s32[]{:T(128)}, s32[256]{0:T(256)S(1)}, bf16[1,256,2048]{2,1,0:T(8,128)(2,1)S(1)}, bf16[512,2,128]{0,2,1:T(8,128)(2,1)S(1)}, bf16[512,2,128]{0,2,1:T(8,128)(2,1)S(1)}) %tuple.38), branch_computations={%region_5.6_spmd, %region_6.9_spmd} | conditional | flops 1097478400 | bytes 31640596 | solution.py:138
  30.0 1.7 %fusion = (f32[256,2,8]{0,2,1:T(8,128)S(1)}, f32[2,512,256,8]{2,1,3,0:T(8,128)S(1)}) fusion(pred[256,512]{0,1:T(8,128)(4,1)S(1)} %iota_compare_fusion, bf16[256,2,8,128]{3,2,1,0:T(8,128)(2,1)S(1)} %bitcast.98, bf16[512,2,128]{0,2,1:T(8,128)(2,1)S(1)} %get-tuple-element.81), kind=kOutput, calls=%fused_computation.2 | convolution fusion | flops 543158272 | bytes 9846784 | tf_op jit(solution)/shard_map/cond/branch_1_fun/while/body/eval_jaxpr/tkgd,skd->tkgs/dot_general | solution.py:57
  31.7 1.7 %fusion.4 = f32[256,2,8]{0,2,1:T(8,128)S(1)} fusion(f32[2,512,256,8]{2,1,3,0:T(8,128)S(1)} %get-tuple-element.88, f32[256,2,8]{0,2,1:T(8,128)S(1)} %broadcast_maximum_fusion, pred[256,512]{0,1:T(8,128)(4,1)S(1)} %iota_compare_fusion), kind=kLoop, calls=%fused_computation.6 | loop fusion | flops 8384512 | bytes 8552448 | tf_op jit(solution)/shard_map/cond/branch_1_fun/while/body/eval_jaxpr/reduce_sum | solution.py:65
  33.5 2.6 %bitcast_add_fusion = f32[256,2,8,128]{3,0,2,1:T(8,128)S(1)} fusion(f32[2,512,256,8]{2,1,3,0:T(8,128)S(1)} %get-tuple-element.88, f32[256,2,8]{0,2,1:T(8,128)S(1)} %broadcast_maximum_fusion, pred[256,512]{0,1:T(8,128)(4,1)S(1)} %iota_compare_fusion, f32[256,2,8]{0,2,1:T(8,128)S(1)} %get-tuple-element.85, bf16[512,2,128]{0,2,1:T(8,128)(2,1)S(1)} %get-tuple-element.82), kind=kOutput, calls=%fused_computation.9 | convolution fusion | flops 545783808 | bytes 10911744 | tf_op jit(solution)/shard_map/cond/branch_1_fun/while/body/eval_jaxpr/tkgs,skd->tkgd/dot_general | solution.py:66
  37.5 1.3 %broadcast_in_dim_reshape.3 = bf16[1,256,2048]{2,1,0:T(8,128)(2,1)} reshape(bf16[256,2,8,128]{3,2,1,0:T(8,128)(2,1)S(1)} %copy.79) | data formatting | bytes 2097152 | tf_op jit(solution)/shard_map/broadcast_in_dim;reshape | solution.py:142
  38.8 1.3 %collective-permute-start.1 = (bf16[1,256,2048]{2,1,0:T(8,128)(2,1)}, bf16[1,256,2048]{2,1,0:T(8,128)(2,1)}, u32[]{:S(2)}, u32[]{:S(2)}) collective-permute-start(bf16[1,256,2048]{2,1,0:T(8,128)(2,1)} %broadcast_in_dim_reshape.3), channel_id=1, source_target_pairs={{3,0},{0,1},{1,2},{2,3},{7,4},{4,5},{5,6},{6,7},{11,8},{8,9},{9,10... | collective-permute-start | bytes 3145736 | tf_op jit(solution)/shard_map/ppermute | solution.py:18
  40.0 4.8 %all-gather = f32[2,1,16]{2,1,0:T(1,128)S(1)} all-gather(f32[1,1,16]{2,1,0:T(1,128)S(1)} %copy.70), channel_id=2, replica_groups=mesh['ctx'=2,'tp'=4,'pp'=4] {'ctx'}, dimensions={0}, use_global_device_ids=true | all-gather | bytes 192 | tf_op jit(solution)/shard_map/all_gather | solution.py:96
  45.4 4.4 %fusion.20 = f32[16,256,128]{1,2,0:T(8,128)} fusion(bf16[256,16,128]{0,2,1:T(8,128)(2,1)S(1)} %bitcast.104, f32[16,256]{1,0:T(8,128)S(1)} %bitcast_add_fusion.3, pred[256,256]{1,0:T(8,128)(4,1)S(1)} %iota_compare_fusion.1, bf16[256,16,128]{2,1,0:T(8,128)(2,1)} %bitcast.49, bf16[256,16,128]{2,1,0:T(8,128)(2,1)S(1)} %bitcast.94), kind=kOutput, calls=%fused_computation.33 | convolution fusion | flops 542113792 | bytes 5324800 | tf_op jit(solution)/shard_map/bhts,bshd->bthd/dot_general | solution.py:35
  49.8 1.1 %all-gather.4.cloned.1.call-done = f32[32,128,128]{2,1,0:T(8,128)} async-done(((f32[16,128,128]{2,1,0:T(8,128)}), f32[32,128,128]{2,1,0:T(8,128)}) %all-gather.4.cloned.1.call-update) | async-done | bytes 2097168 | tf_op jit(solution)/shard_map/all_gather | solution.py:95
  50.9 1.9 %multiply_reduce_fusion = f32[16,128,128]{2,1,0:T(8,128)S(1)} fusion(f32[16,2,128,128]{3,2,0,1:T(8,128)} %bitcast.99, f32[16,2]{0,1:T(2,128)S(1)} %select_bitcast_fusion), kind=kLoop, calls=%fused_computation.24 | loop fusion | flops 786432 | bytes 3145856 | tf_op jit(solution)/shard_map/jh,jhde->hde/dot_general | solution.py:106
  52.8 3.0 %fusion.17 = f32[16,128,256]{2,1,0:T(8,128)S(1)} fusion(f32[16,128,128]{2,1,0:T(8,128)S(1)} %multiply_reduce_fusion, f32[16]{0:T(128)S(1)} %get-tuple-element.91, f32[256,16]{0,1:T(8,128)S(1)} %bitcast.107, bf16[256,16,128]{2,1,0:T(8,128)(2,1)S(1)} %bitcast.95), kind=kOutput, calls=%fused_computation.28 | convolution fusion | flops 806879232 | bytes 4210752 | tf_op jit(solution)/shard_map/bthd,hde->bthe/dot_general | solution.py:107
  55.8 2.8 %multiply_reduce_fusion.1 = (f32[256,16]{0,1:T(8,128)S(1)}, f32[1,256,16,128]{1,3,2,0:T(8,128)S(1)}) fusion(f32[16,128,256]{2,1,0:T(8,128)S(1)} %fusion.17, f32[256,16]{0,1:T(8,128)S(1)} %bitcast.108, bf16[256,16,128]{2,1,0:T(8,128)(2,1)S(1)} %bitcast.96, f32[16,256,128]{1,2,0:T(8,128)S(1)} %copy-done.2), kind=kOutput, calls=%fused_computation.27 | convolution fusion | flops 808448000 | bytes 7372800 | tf_op jit(solution)/shard_map/bthd,bhde->bthe/dot_general | solution.py:49
  58.6 1.9 %copy.74 = f32[1,256,2048]{2,1,0:T(8,128)} copy(f32[1,256,2048]{1,2,0:T(8,128)S(1)} %bitcast.97) | data formatting | bytes 4194304 | tf_op jit(solution)/shard_map/reshape | solution.py:108
  60.6 1.9 %mul.139 = f32[256,16,128]{2,1,0:T(8,128)} broadcast(f32[256,16]{1,0:T(8,128)S(1)} %copy.73), dimensions={0,1} | broadcast | bytes 2113536 | tf_op jit(solution)/shard_map/mul | solution.py:109
  62.6 2.8 %mul.140 = f32[1,256,2048]{2,1,0:T(8,128)} reshape(f32[256,16,128]{2,1,0:T(8,128)} %mul.139) | data formatting | bytes 4194304 | tf_op jit(solution)/shard_map/mul | solution.py:109
  65.4 2.2 %multiply_convert_fusion.1 = bf16[1,256,2048]{2,1,0:T(8,128)(2,1)S(1)} fusion(bf16[1,256,2048]{2,1,0:T(8,128)(2,1)S(1)} %copy-done.8, f32[1,256,2048]{2,1,0:T(8,128)S(1)} %copy-done.1, f32[1,256,2048]{2,1,0:T(8,128)} %mul.140, f32[2048]{0:T(1024)S(1)} %bitcast.114), kind=kLoop, calls=%fused_computation.26 | loop fusion | flops 4194304 | bytes 6299648 | tf_op jit(solution)/shard_map/convert_element_type | solution.py:114
  67.6 1.7 %collective-permute-start = (bf16[1,256,2048]{2,1,0:T(8,128)(2,1)S(1)}, bf16[1,256,2048]{2,1,0:T(8,128)(2,1)S(1)}, u32[]{:S(2)}, u32[]{:S(2)}) collective-permute-start(bf16[1,256,2048]{2,1,0:T(8,128)(2,1)S(1)} %multiply_convert_fusion.1), channel_id=1, source_target_pairs={{3,0},{0,1},{1,2},{2,3},{7,4},{4,5},{5,6},{6,7},{11,8},{8,9},{9,10... | collective-permute-start | bytes 3145736 | tf_op jit(solution)/shard_map/ppermute | solution.py:18
  69.3 25.4 %collective-permute-done = bf16[1,256,2048]{2,1,0:T(8,128)(2,1)S(1)} collective-permute-done((bf16[1,256,2048]{2,1,0:T(8,128)(2,1)S(1)}, bf16[1,256,2048]{2,1,0:T(8,128)(2,1)S(1)}, u32[]{:S(2)}, u32[]{:S(2)}) %collective-permute-start) | collective-permute-done | bytes 1048608 | tf_op jit(solution)/shard_map/ppermute | solution.py:18
  95.6 2.3 %copy.140 = bf16[1,256,2048]{2,1,0:T(8,128)(2,1)} copy(bf16[1,256,2048]{2,1,0:T(8,128)(2,1)} %collective-permute-done.1) | data formatting | bytes 2097152
  (63 shorter events, 5.7 us)
Async XLA Ops:
  7.2 0.7 copy-start
  7.2 3.6 %copy-start.3 = (bf16[1,256,2048]{2,1,0:T(8,128)(2,1)S(1)}, bf16[1,256,2048]{2,1,0:T(8,128)(2,1)}, u32[]{:S(2)}) copy-start(bf16[1,256,2048]{2,1,0:T(8,128)(2,1)} %param.13) | copy-start | bytes 3145732
  7.2 43.7 %all-gather.4.cloned.1.call-start = ((), (), s32[]{:S(2)}) async-start(), calls=%async_computation | async-start | bytes 3145728 | tf_op jit(solution)/shard_map/all_gather | solution.py:95
  10.8 4.1 %copy-start.6 = (bf16[1,256,2048]{1,2,0:T(8,128)(2,1)}, bf16[1,256,2048]{1,2,0:T(8,128)(2,1)S(1)}, u32[]{:S(2)}) copy-start(bf16[1,256,2048]{1,2,0:T(8,128)(2,1)S(1)} %copy.98) | copy-start | bytes 3145732
  12.1 2.9 %copy-start.9 = (bf16[1,256,256]{2,1,0:T(8,128)(2,1)S(1)}, bf16[1,256,256]{2,1,0:T(8,128)(2,1)}, u32[]{:S(2)}) copy-start(bf16[1,256,256]{2,1,0:T(8,128)(2,1)} %param.18) | copy-start | bytes 393220
  12.1 3.0 %copy-start.10 = (bf16[1,256,256]{2,1,0:T(8,128)(2,1)S(1)}, bf16[1,256,256]{2,1,0:T(8,128)(2,1)}, u32[]{:S(2)}) copy-start(bf16[1,256,256]{2,1,0:T(8,128)(2,1)} %param.19) | copy-start | bytes 393220
  12.1 17.6 %copy-start.4 = (bf16[1,256,2048]{2,1,0:T(8,128)(2,1)S(1)}, bf16[1,256,2048]{2,1,0:T(8,128)(2,1)}, u32[]{:S(2)}) copy-start(bf16[1,256,2048]{2,1,0:T(8,128)(2,1)} %param.17) | copy-start | bytes 3145732
  36.8 8.1 %copy-start.5 = (bf16[1,256,2048]{2,1,0:T(8,128)(2,1)S(1)}, bf16[1,256,2048]{2,1,0:T(8,128)(2,1)}, u32[]{:S(2)}) copy-start(bf16[1,256,2048]{2,1,0:T(8,128)(2,1)} %param.11) | copy-start | bytes 3145732
  37.5 7.9 %copy-start.7 = (bf16[1,256,2048]{1,2,0:T(8,128)(2,1)S(1)}, bf16[1,256,2048]{1,2,0:T(8,128)(2,1)}, u32[]{:S(2)}) copy-start(bf16[1,256,2048]{1,2,0:T(8,128)(2,1)} %copy-done.6) | copy-start | bytes 3145732
  38.8 30.5 %collective-permute-start.1 = (bf16[1,256,2048]{2,1,0:T(8,128)(2,1)}, bf16[1,256,2048]{2,1,0:T(8,128)(2,1)}, u32[]{:S(2)}, u32[]{:S(2)}) collective-permute-start(bf16[1,256,2048]{2,1,0:T(8,128)(2,1)} %broadcast_in_dim_reshape.3), channel_id=1, source_target_pairs={{3,0},{0,1},{1,2},{2,3},{7,4},{4,5},{5,6},{6,7},{11,8},{8,9},{9,10... | collective-permute-start | bytes 3145736 | tf_op jit(solution)/shard_map/ppermute | solution.py:18
  52.8 3.0 %copy-start.2 = (f32[16,256,128]{1,2,0:T(8,128)S(1)}, f32[16,256,128]{1,2,0:T(8,128)}, u32[]{:S(2)}) copy-start(f32[16,256,128]{1,2,0:T(8,128)} %fusion.20) | copy-start | bytes 6291460
  62.5 2.8 %copy-start.1 = (f32[1,256,2048]{2,1,0:T(8,128)S(1)}, f32[1,256,2048]{2,1,0:T(8,128)}, u32[]{:S(2)}) copy-start(f32[1,256,2048]{2,1,0:T(8,128)} %copy.74) | copy-start | bytes 6291460
  62.5 2.8 %copy-start.8 = (bf16[1,256,2048]{2,1,0:T(8,128)(2,1)S(1)}, bf16[1,256,2048]{2,1,0:T(8,128)(2,1)}, u32[]{:S(2)}) copy-start(bf16[1,256,2048]{2,1,0:T(8,128)(2,1)} %param.15) | copy-start | bytes 3145732
  62.6 2.8 %copy-start.11 = (f32[1,2048]{1,0:T(1,128)S(1)}, f32[1,2048]{1,0:T(1,128)}, u32[]{:S(2)}) copy-start(f32[1,2048]{1,0:T(1,128)} %param.16) | copy-start | bytes 24580
  67.6 27.1 %collective-permute-start = (bf16[1,256,2048]{2,1,0:T(8,128)(2,1)S(1)}, bf16[1,256,2048]{2,1,0:T(8,128)(2,1)S(1)}, u32[]{:S(2)}, u32[]{:S(2)}) collective-permute-start(bf16[1,256,2048]{2,1,0:T(8,128)(2,1)S(1)} %multiply_convert_fusion.1), channel_id=1, source_target_pairs={{3,0},{0,1},{1,2},{2,3},{7,4},{4,5},{5,6},{6,7},{11,8},{8,9},{9,10... | collective-permute-start | bytes 3145736 | tf_op jit(solution)/shard_map/ppermute | solution.py:18
Sparse Core Ops, SparseCore 0:
  15.1 35.8 all-gather.3
where the time goes:
time: 105 us
  waiting for transfers between devices  26.6 us (25%)
  blocking collectives  19.3 us (18%)
  matrix products  17.2 us (16%)
  local copies, waits for them, and re-layouts  16.8 us (16%)
  between operations  14.3 us (14%)
  other arithmetic  7.62 us (7%)
  starting transfers between devices  2.99 us (3%)
    ppermute x2, waiting for transfers between devices, passed_along(): return lax.ppermute(block, axis, route)  25.4 us
    all_gather x1, blocking collectives, local(): value_piece = lax.all_gather(value_rows, 'ctx', axis=0, tiled=True)  7.36 us
    all_gather x1, blocking collectives, local(): key_piece = lax.all_gather(key_rows, 'ctx', axis=0, tiled=True)  7.09 us
    unnamed x32, local copies, waits for them, and re-layouts  5.69 us
    all_gather x1, blocking collectives, local(): lax.all_gather(device_log[None, :], 'ctx', axis=0, tiled=True)  4.82 us
    mul x2, local copies, waits for them, and re-layouts, local(): mixture * lax.rsqrt(jnp.mean(mixture * mixture, axis=-1, keepdims=True) +...  4.77 us
    dot_general x1, matrix products, lightning_local(): jnp.einsum('bhts,bshd->bthd', weights, values_all, preferred_element_type...  4.43 us
    dot_general x1, matrix products, local(): jnp.einsum('bthd,hde->bthe', carried, incoming, precision=lax.Precision.H...  2.96 us
  transfers between devices with their start and end apart: 3, of which 2 were waited for; matrix products, arithmetic and copies ran while one was open for 29% of the time, Pallas kernels for 0%

commit v1 on v0

--- a/solution.py
+++ b/solution.py
@@ -10,6 +10,12 @@
 BLK = 256
 epsilon = 1e-06
 lowest = -1e30
+
+
+def make_lots_all(vector, mat):
+    z1 = jax.lax.all_gather(jnp.concatenate([vector, mat], 1), "ctx", axis=0, tiled=True)
+    y1 = jnp.split(z1, [vector.shape[1]], axis=1)
+    return y1
 
 
 def passed_along(block, axis, distance):
@@ -117,8 +123,7 @@
     value_rows = soft_value[0].reshape(length, kv_count, HD)
     row_pos = position * length + lax.iota(jnp.int32, length)
     last_row = position * length + length - 1
-    key_piece = lax.all_gather(key_rows, "ctx", axis=0, tiled=True)
-    value_piece = lax.all_gather(value_rows, "ctx", axis=0, tiled=True)
+    key_piece, value_piece = make_lots_all(key_rows, value_rows)
     piece_rows = key_piece.shape[0]
     stride = math.gcd(piece_rows, 512)
 

time: 105 us -> 105 us (level)
  blocking collectives: 19.3 us -> 14.3 us
  waiting for transfers between devices: 26.6 us -> 30.7 us
    all_gather x2 -> x1, blocking collectives: 14.5 us -> 9.91 us  [make_lots_all(): jax.lax.all_gather(jnp.concatenate([vector, mat], 1), 'ctx', axis=0, tile...]
    all_gather x1, waiting for transfers between devices: 1.15 us -> 5.45 us  [local(): lax.all_gather(closing[None], 'ctx', axis=0, tiled=True)]
  transfers between devices with their start and end apart: 3 -> 3, of which waited for: 2 -> 2; matrix products, arithmetic and copies ran while one was open for 29% -> 30% of each run, Pallas kernels for 0% -> 0%
where the time goes in v1:
time: 105 us; the launch traced here: 104 us
  waiting for transfers between devices  30.7 us (29%)
  local copies, waits for them, and re-layouts  17.1 us (16%)
  matrix products  17 us (16%)
  blocking collectives  14.3 us (14%)
  between operations  14.3 us (14%)
  other arithmetic  7.65 us (7%)
  starting transfers between devices  3.41 us (3%)
    ppermute x2, waiting for transfers between devices, passed_along(): return lax.ppermute(block, axis, route)  25.2 us
    all_gather x1, blocking collectives, make_lots_all(): jax.lax.all_gather(jnp.concatenate([vector, mat], 1), 'ctx', axis=0, tile...  9.91 us
    unnamed x32, local copies, waits for them, and re-layouts  5.69 us
    all_gather x1, waiting for transfers between devices, local(): lax.all_gather(closing[None], 'ctx', axis=0, tiled=True)  5.45 us
    mul x2, local copies, waits for them, and re-layouts, local(): mixture * lax.rsqrt(jnp.mean(mixture * mixture, axis=-1, keepdims=True) +...  4.77 us
    dot_general x1, matrix products, lightning_local(): jnp.einsum('bhts,bshd->bthd', weights, values_all, preferred_element_type...  4.43 us
    all_gather x1, blocking collectives, local(): lax.all_gather(device_log[None, :], 'ctx', axis=0, tiled=True)  4.39 us
    ppermute x2, starting transfers between devices, passed_along(): return lax.ppermute(block, axis, route)  3.37 us
  transfers between devices with their start and end apart: 3, of which 2 were waited for; matrix products, arithmetic and copies ran while one was open for 30% of the time, Pallas kernels for 0%

profile of v1, /device:TPU:0, one launch (start us, length us, event | category | flops | bytes accessed | tf_op | source)
XLA Modules:
  0.0 104.4 jit_solution(17386262384960449618)
XLA Ops:
  9.3 1.5 %copy.91 = bf16[1,256,2048]{1,2,0:T(8,128)(2,1)S(1)} copy(bf16[1,256,2048]{2,1,0:T(8,128)(2,1)} %param.12) | data formatting | bytes 2097152 | tf_op jit(solution)/shard_map/reshape.8
  10.8 1.3 %copy.97 = bf16[32,8,16,128]{3,2,1,0:T(8,128)(2,1)} copy(bf16[32,8,16,128]{3,1,2,0:T(8,128)(2,1)S(1)} %bitcast.100) | data formatting | bytes 2097152
  12.1 2.8 %convolution_add_fusion = f32[16,128,128]{2,1,0:T(8,128)} fusion(bf16[256,16,128]{0,2,1:T(8,128)(2,1)S(1)} %bitcast.103, f32[256,16]{0,1:T(8,128)S(1)} %bitcast.113, bf16[256,16,128]{2,1,0:T(8,128)(2,1)} %bitcast.49, f32[16]{0:T(128)S(1)} %get-tuple-element.89), kind=kOutput, calls=%fused_computation.34 | convolution fusion | flops 136052736 | bytes 3162176 | tf_op jit(solution)/shard_map/bshd,bshe->bhde/dot_general | solution.py:45
  15.2 9.9 %all_gather.11 = bf16[512,4,128]{0,2,1:T(8,128)(2,1)S(1)} all-gather(bf16[256,4,128]{0,2,1:T(8,128)(2,1)S(1)} %pad_maximum_fusion), channel_id=1, replica_groups=mesh['ctx'=2,'tp'=4,'pp'=4] {'ctx'}, dimensions={0}, use_global_device_ids=true | all-gather | bytes 786432 | tf_op jit(solution)/shard_map/all_gather | solution.py:16
  25.1 6.4 %conditional.1 = (f32[256,2,8]{0,2,1:T(8,128)S(1)}, f32[256,2,8,128]{3,0,2,1:T(8,128)S(1)}) conditional(s32[]{:T(128)} %convert_element_type.48, () %tuple.20, (s32[]{:T(128)}, s32[256]{0:T(256)S(1)}, bf16[512,4,128]{0,2,1:T(8,128)(2,1)S(1)}, bf16[1,256,2048]{2,1,0:T(8,128)(2,1)S(1)}) %tuple.38), branch_computations={%region_5.6_spmd, %region_6.9_spmd} | conditional | flops 1097478400 | bytes 32689172 | solution.py:143
  25.8 1.5 %fusion = (f32[256,2,8]{0,2,1:T(8,128)S(1)}, f32[2,512,256,8]{2,1,3,0:T(8,128)S(1)}) fusion(pred[256,512]{0,1:T(8,128)(4,1)S(1)} %iota_compare_fusion, bf16[256,2,8,128]{3,2,1,0:T(8,128)(2,1)S(1)} %bitcast.98, bf16[512,4,128]{2,0,1:T(8,128)(2,1)S(1)} %copy.75), kind=kOutput, calls=%fused_computation.2 | convolution fusion | flops 543158272 | bytes 9846784 | tf_op jit(solution)/shard_map/cond/branch_1_fun/while/body/eval_jaxpr/tkgd,skd->tkgs/dot_general | solution.py:63
  27.3 1.7 %fusion.4 = f32[256,2,8]{0,2,1:T(8,128)S(1)} fusion(f32[2,512,256,8]{2,1,3,0:T(8,128)S(1)} %get-tuple-element.85, f32[256,2,8]{0,2,1:T(8,128)S(1)} %broadcast_maximum_fusion, pred[256,512]{0,1:T(8,128)(4,1)S(1)} %iota_compare_fusion), kind=kLoop, calls=%fused_computation.6 | loop fusion | flops 8384512 | bytes 8552448 | tf_op jit(solution)/shard_map/cond/branch_1_fun/while/body/eval_jaxpr/reduce_sum | solution.py:71
  29.0 2.5 %bitcast_add_fusion = f32[256,2,8,128]{3,0,2,1:T(8,128)S(1)} fusion(f32[2,512,256,8]{2,1,3,0:T(8,128)S(1)} %get-tuple-element.85, f32[256,2,8]{0,2,1:T(8,128)S(1)} %broadcast_maximum_fusion, pred[256,512]{0,1:T(8,128)(4,1)S(1)} %iota_compare_fusion, f32[256,2,8]{0,2,1:T(8,128)S(1)} %get-tuple-element.82, bf16[512,4,128]{2,0,1:T(8,128)(2,1)S(1)} %copy.75), kind=kOutput, calls=%fused_computation.9 | convolution fusion | flops 545783808 | bytes 10911744 | tf_op jit(solution)/shard_map/cond/branch_1_fun/while/body/eval_jaxpr/tkgs,skd->tkgd/dot_general | solution.py:72
  33.0 1.3 %broadcast_in_dim_reshape.3 = bf16[1,256,2048]{2,1,0:T(8,128)(2,1)} reshape(bf16[256,2,8,128]{3,2,1,0:T(8,128)(2,1)S(1)} %copy.76) | data formatting | bytes 2097152 | tf_op jit(solution)/shard_map/broadcast_in_dim;reshape | solution.py:147
  34.3 1.8 %collective-permute-start.1 = (bf16[1,256,2048]{2,1,0:T(8,128)(2,1)}, bf16[1,256,2048]{2,1,0:T(8,128)(2,1)}, u32[]{:S(2)}, u32[]{:S(2)}) collective-permute-start(bf16[1,256,2048]{2,1,0:T(8,128)(2,1)} %broadcast_in_dim_reshape.3), channel_id=1, source_target_pairs={{3,0},{0,1},{1,2},{2,3},{7,4},{4,5},{5,6},{6,7},{11,8},{8,9},{9,10... | collective-permute-start | bytes 3145736 | tf_op jit(solution)/shard_map/ppermute | solution.py:24
  36.1 4.4 %all-gather = f32[2,1,16]{2,1,0:T(1,128)S(1)} all-gather(f32[1,1,16]{2,1,0:T(1,128)S(1)} %copy.68), channel_id=2, replica_groups=mesh['ctx'=2,'tp'=4,'pp'=4] {'ctx'}, dimensions={0}, use_global_device_ids=true | all-gather | bytes 192 | tf_op jit(solution)/shard_map/all_gather | solution.py:102
  41.0 4.4 %fusion.18 = f32[16,256,128]{1,2,0:T(8,128)} fusion(bf16[256,16,128]{0,2,1:T(8,128)(2,1)S(1)} %bitcast.104, f32[16,256]{1,0:T(8,128)S(1)} %bitcast_add_fusion.3, pred[256,256]{1,0:T(8,128)(4,1)S(1)} %iota_compare_fusion.1, bf16[256,16,128]{2,1,0:T(8,128)(2,1)} %bitcast.49, bf16[256,16,128]{2,1,0:T(8,128)(2,1)S(1)} %bitcast.94), kind=kOutput, calls=%fused_computation.33 | convolution fusion | flops 542113792 | bytes 5324800 | tf_op jit(solution)/shard_map/bhts,bshd->bthd/dot_general | solution.py:41
  45.4 5.5 %all-gather.4.cloned.1.call-done = f32[32,128,128]{2,1,0:T(8,128)} async-done(((f32[16,128,128]{2,1,0:T(8,128)}), f32[32,128,128]{2,1,0:T(8,128)}) %all-gather.4.cloned.1.call-update) | async-done | bytes 2097168 | tf_op jit(solution)/shard_map/all_gather | solution.py:101
  50.9 1.9 %multiply_reduce_fusion = f32[16,128,128]{2,1,0:T(8,128)S(1)} fusion(f32[16,2,128,128]{3,2,0,1:T(8,128)} %bitcast.99, f32[16,2]{0,1:T(2,128)S(1)} %select_bitcast_fusion), kind=kLoop, calls=%fused_computation.24 | loop fusion | flops 786432 | bytes 3145856 | tf_op jit(solution)/shard_map/jh,jhde->hde/dot_general | solution.py:112
  52.8 3.0 %fusion.15 = f32[16,128,256]{2,1,0:T(8,128)S(1)} fusion(f32[16,128,128]{2,1,0:T(8,128)S(1)} %multiply_reduce_fusion, f32[16]{0:T(128)S(1)} %get-tuple-element.88, f32[256,16]{0,1:T(8,128)S(1)} %bitcast.107, bf16[256,16,128]{2,1,0:T(8,128)(2,1)S(1)} %bitcast.95), kind=kOutput, calls=%fused_computation.28 | convolution fusion | flops 806879232 | bytes 4210752 | tf_op jit(solution)/shard_map/bthd,hde->bthe/dot_general | solution.py:113
  55.8 2.8 %multiply_reduce_fusion.1 = (f32[256,16]{0,1:T(8,128)S(1)}, f32[1,256,16,128]{1,3,2,0:T(8,128)S(1)}) fusion(f32[16,128,256]{2,1,0:T(8,128)S(1)} %fusion.15, f32[256,16]{0,1:T(8,128)S(1)} %bitcast.108, bf16[256,16,128]{2,1,0:T(8,128)(2,1)S(1)} %bitcast.96, f32[16,256,128]{1,2,0:T(8,128)S(1)} %copy-done.2), kind=kOutput, calls=%fused_computation.27 | convolution fusion | flops 808448000 | bytes 7372800 | tf_op jit(solution)/shard_map/bthd,bhde->bthe/dot_general | solution.py:55
  58.6 1.9 %copy.72 = f32[1,256,2048]{2,1,0:T(8,128)} copy(f32[1,256,2048]{1,2,0:T(8,128)S(1)} %bitcast.97) | data formatting | bytes 4194304 | tf_op jit(solution)/shard_map/reshape | solution.py:114
  60.5 1.9 %mul.139 = f32[256,16,128]{2,1,0:T(8,128)} broadcast(f32[256,16]{1,0:T(8,128)S(1)} %copy.71), dimensions={0,1} | broadcast | bytes 2113536 | tf_op jit(solution)/shard_map/mul | solution.py:115
  62.5 2.8 %mul.140 = f32[1,256,2048]{2,1,0:T(8,128)} reshape(f32[256,16,128]{2,1,0:T(8,128)} %mul.139) | data formatting | bytes 4194304 | tf_op jit(solution)/shard_map/mul | solution.py:115
  65.3 2.2 %multiply_convert_fusion.1 = bf16[1,256,2048]{2,1,0:T(8,128)(2,1)S(1)} fusion(bf16[1,256,2048]{2,1,0:T(8,128)(2,1)S(1)} %copy-done.8, f32[1,256,2048]{2,1,0:T(8,128)S(1)} %copy-done.1, f32[1,256,2048]{2,1,0:T(8,128)} %mul.140, f32[2048]{0:T(1024)S(1)} %bitcast.114), kind=kLoop, calls=%fused_computation.26 | loop fusion | flops 4194304 | bytes 6299648 | tf_op jit(solution)/shard_map/convert_element_type | solution.py:120
  67.5 1.5 %collective-permute-start = (bf16[1,256,2048]{2,1,0:T(8,128)(2,1)S(1)}, bf16[1,256,2048]{2,1,0:T(8,128)(2,1)S(1)}, u32[]{:S(2)}, u32[]{:S(2)}) collective-permute-start(bf16[1,256,2048]{2,1,0:T(8,128)(2,1)S(1)} %multiply_convert_fusion.1), channel_id=1, source_target_pairs={{3,0},{0,1},{1,2},{2,3},{7,4},{4,5},{5,6},{6,7},{11,8},{8,9},{9,10... | collective-permute-start | bytes 3145736 | tf_op jit(solution)/shard_map/ppermute | solution.py:24
  69.1 25.2 %collective-permute-done = bf16[1,256,2048]{2,1,0:T(8,128)(2,1)S(1)} collective-permute-done((bf16[1,256,2048]{2,1,0:T(8,128)(2,1)S(1)}, bf16[1,256,2048]{2,1,0:T(8,128)(2,1)S(1)}, u32[]{:S(2)}, u32[]{:S(2)}) %collective-permute-start) | collective-permute-done | bytes 1048608 | tf_op jit(solution)/shard_map/ppermute | solution.py:24
  94.3 1.0 copy.132
  95.3 2.3 %copy.133 = bf16[1,256,2048]{2,1,0:T(8,128)(2,1)} copy(bf16[1,256,2048]{2,1,0:T(8,128)(2,1)} %collective-permute-done.1) | data formatting | bytes 2097152
  (64 shorter events, 5.0 us)
Async XLA Ops:
  7.2 0.7 copy-start
  7.2 3.6 %copy-start.3 = (bf16[1,256,2048]{2,1,0:T(8,128)(2,1)S(1)}, bf16[1,256,2048]{2,1,0:T(8,128)(2,1)}, u32[]{:S(2)}) copy-start(bf16[1,256,2048]{2,1,0:T(8,128)(2,1)} %param.13) | copy-start | bytes 3145732
  7.2 43.7 %all-gather.4.cloned.1.call-start = ((), (), s32[]{:S(2)}) async-start(), calls=%async_computation | async-start | bytes 3145728 | tf_op jit(solution)/shard_map/all_gather | solution.py:101
  10.8 4.1 %copy-start.6 = (bf16[1,256,2048]{1,2,0:T(8,128)(2,1)}, bf16[1,256,2048]{1,2,0:T(8,128)(2,1)S(1)}, u32[]{:S(2)}) copy-start(bf16[1,256,2048]{1,2,0:T(8,128)(2,1)S(1)} %copy.91) | copy-start | bytes 3145732
  12.1 2.9 %copy-start.9 = (bf16[1,256,256]{2,1,0:T(8,128)(2,1)S(1)}, bf16[1,256,256]{2,1,0:T(8,128)(2,1)}, u32[]{:S(2)}) copy-start(bf16[1,256,256]{2,1,0:T(8,128)(2,1)} %param.19) | copy-start | bytes 393220
  12.1 3.0 %copy-start.10 = (bf16[1,256,256]{2,1,0:T(8,128)(2,1)S(1)}, bf16[1,256,256]{2,1,0:T(8,128)(2,1)}, u32[]{:S(2)}) copy-start(bf16[1,256,256]{2,1,0:T(8,128)(2,1)} %param.18) | copy-start | bytes 393220
  14.9 10.3 %copy-start.4 = (bf16[1,256,2048]{2,1,0:T(8,128)(2,1)S(1)}, bf16[1,256,2048]{2,1,0:T(8,128)(2,1)}, u32[]{:S(2)}) copy-start(bf16[1,256,2048]{2,1,0:T(8,128)(2,1)} %param.17) | copy-start | bytes 3145732
  32.3 8.3 %copy-start.5 = (bf16[1,256,2048]{2,1,0:T(8,128)(2,1)S(1)}, bf16[1,256,2048]{2,1,0:T(8,128)(2,1)}, u32[]{:S(2)}) copy-start(bf16[1,256,2048]{2,1,0:T(8,128)(2,1)} %param.11) | copy-start | bytes 3145732
  33.0 8.0 %copy-start.7 = (bf16[1,256,2048]{1,2,0:T(8,128)(2,1)S(1)}, bf16[1,256,2048]{1,2,0:T(8,128)(2,1)}, u32[]{:S(2)}) copy-start(bf16[1,256,2048]{1,2,0:T(8,128)(2,1)} %copy-done.6) | copy-start | bytes 3145732
  34.3 34.8 %collective-permute-start.1 = (bf16[1,256,2048]{2,1,0:T(8,128)(2,1)}, bf16[1,256,2048]{2,1,0:T(8,128)(2,1)}, u32[]{:S(2)}, u32[]{:S(2)}) collective-permute-start(bf16[1,256,2048]{2,1,0:T(8,128)(2,1)} %broadcast_in_dim_reshape.3), channel_id=1, source_target_pairs={{3,0},{0,1},{1,2},{2,3},{7,4},{4,5},{5,6},{6,7},{11,8},{8,9},{9,10... | collective-permute-start | bytes 3145736 | tf_op jit(solution)/shard_map/ppermute | solution.py:24
  52.8 3.0 %copy-start.2 = (f32[16,256,128]{1,2,0:T(8,128)S(1)}, f32[16,256,128]{1,2,0:T(8,128)}, u32[]{:S(2)}) copy-start(f32[16,256,128]{1,2,0:T(8,128)} %fusion.18) | copy-start | bytes 6291460
  62.5 2.8 %copy-start.1 = (f32[1,256,2048]{2,1,0:T(8,128)S(1)}, f32[1,256,2048]{2,1,0:T(8,128)}, u32[]{:S(2)}) copy-start(f32[1,256,2048]{2,1,0:T(8,128)} %copy.72) | copy-start | bytes 6291460
  62.5 2.8 %copy-start.8 = (bf16[1,256,2048]{2,1,0:T(8,128)(2,1)S(1)}, bf16[1,256,2048]{2,1,0:T(8,128)(2,1)}, u32[]{:S(2)}) copy-start(bf16[1,256,2048]{2,1,0:T(8,128)(2,1)} %param.15) | copy-start | bytes 3145732
  62.5 2.8 %copy-start.11 = (f32[1,2048]{1,0:T(1,128)S(1)}, f32[1,2048]{1,0:T(1,128)}, u32[]{:S(2)}) copy-start(f32[1,2048]{1,0:T(1,128)} %param.16) | copy-start | bytes 24580
  67.5 26.8 %collective-permute-start = (bf16[1,256,2048]{2,1,0:T(8,128)(2,1)S(1)}, bf16[1,256,2048]{2,1,0:T(8,128)(2,1)S(1)}, u32[]{:S(2)}, u32[]{:S(2)}) collective-permute-start(bf16[1,256,2048]{2,1,0:T(8,128)(2,1)S(1)} %multiply_convert_fusion.1), channel_id=1, source_target_pairs={{3,0},{0,1},{1,2},{2,3},{7,4},{4,5},{5,6},{6,7},{11,8},{8,9},{9,10... | collective-permute-start | bytes 3145736 | tf_op jit(solution)/shard_map/ppermute | solution.py:24
Sparse Core Ops, SparseCore 0:
  15.0 35.8 all-gather.3
